TPU v7x, 512 devices: a whole 4x4x16 slice. The times are simulated.
512 devices in a mesh: row: 32 (over z, core), col: 16 (over y, x).
Axes of the slice: x: 4, y: 4, z: 16, core: 2. Of those that a mesh axis runs over, the one named last changes fastest.
Arguments:
- tokens: bfloat16 [512, 16384], P('col', 'row'), may hold values from -6 to 6
- query_weight: bfloat16 [16384, 8192], P('row', 'col'), may hold values from -0.09375 to 0.09375
- keyval_weight: bfloat16 [16384, 2048], P('row', 'col'), may hold values from -0.09375 to 0.09375
Outputs:
- query_proj: bfloat16 [512, 8192], P('row', 'col')
- query_code: bfloat16 [16384, 8192], P('row', 'col')
- query_scale: float32 [128, 64], P('row', 'col')
- keyval_code: bfloat16 [16384, 2048], P('row', 'col')
- keyval_scale: float32 [128, 16], P('row', 'col')
All inputs are finite; a program needn't handle non-finite values. Where the computation divides by a largest or mean magnitude, that divisor is 1e-20 or more.
Results may differ from a plain program's by a relative error of at most 0.0095.
Values may be sent and summed in bfloat16 or wider, within the bound.
No kernel may reach another device: no remote copies, remote signals or barrier semaphores. Data moves between devices by JAX's collectives and lax.ppermute only.
A program may use at most 64 MiB of HBM per device.

v0:
```python
import math
import jax
import jax.numpy as jnp
from jax import lax
from jax.sharding import PartitionSpec as P

BLOCK = 128
QSTEPS = 4
EPSILON = 1e-06
SOFTNESS = 0.9
TWO_PI = 2.0 * math.pi


def soften(argument):
    return argument - SOFTNESS * jnp.sin(TWO_PI * argument) / TWO_PI


def block_codes(weight, smooth):
    smoothed = weight.astype(jnp.float32) * smooth[:, None]
    height, breadth = smoothed.shape
    tile_view = smoothed.reshape(height // BLOCK, BLOCK, breadth // BLOCK, BLOCK)
    scales = (jnp.max(jnp.abs(tile_view), axis=(1, 3)) + EPSILON) / QSTEPS
    encoded = (
        soften(tile_view / scales[:, None, :, None]).reshape(height, breadth).astype(jnp.bfloat16)
    )
    return (encoded, scales)


def token_encode(x_smooth, row_peak):
    token_scale = ((row_peak + EPSILON) / QSTEPS).astype(jnp.bfloat16)
    encoded = soften(x_smooth / token_scale.astype(jnp.float32)[:, None]).astype(jnp.bfloat16)
    return (encoded, token_scale)


def body(tokens, query_weight, keyval_weight):
    act_local = jnp.max(jnp.abs(tokens), axis=0).astype(jnp.float32)
    weight_local = jnp.maximum(
        jnp.max(jnp.abs(query_weight), axis=1), jnp.max(jnp.abs(keyval_weight), axis=1)
    ).astype(jnp.float32)
    act_peak, weight_peak = lax.pmax((act_local, weight_local), "col")
    smooth = jnp.sqrt((act_peak + EPSILON) / (weight_peak + EPSILON))
    query_code, query_scale = block_codes(query_weight, smooth)
    keyval_code, keyval_scale = block_codes(keyval_weight, smooth)
    x_smooth = tokens.astype(jnp.float32) / smooth[None, :]
    row_peak = lax.pmax(jnp.max(jnp.abs(x_smooth), axis=1), "row")
    local_code, local_scale = token_encode(x_smooth, row_peak)
    x_code, token_scale = (
        lax.all_gather(local_code, "col", axis=0, tiled=True),
        lax.all_gather(local_scale, "col", axis=0, tiled=True),
    )
    column_scale = jnp.repeat(query_scale, BLOCK, axis=1)
    block_total = query_code.shape[0] // BLOCK
    out_width = query_code.shape[1]
    own_rows = x_code.shape[0] // lax.axis_size("row")
    scale_rows = token_scale.astype(jnp.float32)

    def add_block(block_index, running):
        code_block = lax.dynamic_slice_in_dim(x_code, block_index * BLOCK, BLOCK, 1)
        weight_block = lax.dynamic_slice_in_dim(query_code, block_index * BLOCK, BLOCK, 0)
        scale_row = lax.dynamic_slice_in_dim(column_scale, block_index, 1, 0)
        product = jnp.dot(code_block, weight_block, preferred_element_type=jnp.float32)
        return running + product * scale_row

    running = lax.fori_loop(
        0,
        block_total,
        add_block,
        jnp.zeros((own_rows * lax.axis_size("row"), out_width), jnp.float32),
    )
    query_proj = lax.psum_scatter(
        running * scale_rows[:, None], "row", scatter_dimension=0, tiled=True
    ).astype(jnp.bfloat16)
    return (query_proj, query_code, query_scale, keyval_code, keyval_scale)


def solution(mesh):
    in_specs = (P("col", "row"), P("row", "col"), P("row", "col"))
    out_specs = (
        P("row", "col"),
        P("row", "col"),
        P("row", "col"),
        P("row", "col"),
        P("row", "col"),
    )
    return jax.shard_map(body, mesh=mesh, in_specs=in_specs, out_specs=out_specs, check_vma=False)
```

profile of v0, /device:TPU:2, one launch (start us, length us, event | category | flops | bytes accessed | tf_op | source)
XLA Modules:
  0.0 286.5 jit_solution(13215520289935664740)
XLA Ops:
  7.2 1.3 abs_reduce_fusion
  8.5 1.0 abs_reduce_fusion.2
  9.6 41.3 %all-reduce.1 = (f32[512]{0:T(512)S(1)}, f32[512]{0:T(512)S(1)}) all-reduce(f32[512]{0:T(512)S(1)} %maximum_convert_fusion, bf16[512]{0:T(512)(128)(2,1)S(1)} %abs_reduce_fusion.3), channel_id=1, replica_groups=mesh['row'=32,'col'=16] {'col'}, use_global_device_ids=true, to_apply=%region_4.0 | all-reduce | flops 1024 | bytes 7168 | tf_op jit(solution)/shard_map/pmax | solution.py:40
  51.2 1.3 abs.29
  52.6 1.5 reduce_max.65
  54.2 0.5 copy-done.4
  54.9 4.0 %subtract_convert_fusion = bf16[512,512]{1,0:T(8,128)(2,1)S(1)} fusion(f32[64,8,4,128]{3,2,1,0:T(4,128)S(1)} %bitcast.21, bf16[512,512]{1,0:T(8,128)(2,1)S(1)} %copy-done, f32[512]{0:T(512)S(1)} %fusion.7), kind=kLoop, calls=%fused_computation.7 | loop fusion | flops 1835008 | bytes 2099200 | tf_op jit(solution)/shard_map/convert_element_type | solution.py:24
  58.9 47.3 %pmax.23 = f32[32]{0:T(128)S(1)} all-reduce(f32[32]{0:T(128)S(1)} %fusion.6), channel_id=1, replica_groups=mesh['row'=32,'col'=16] {'row'}, use_global_device_ids=true, to_apply=%region_6.0 | all-reduce | flops 32 | bytes 256 | tf_op jit(solution)/shard_map/pmax | solution.py:45
  106.2 0.3 subtract_convert_fusion.2
  106.6 25.4 %all_gather.6 = bf16[512,512]{1,0:T(8,128)(2,1)S(1)} all-gather(bf16[32,512]{1,0:T(8,128)(2,1)S(1)} %subtract_convert_fusion.2), channel_id=1, replica_groups=mesh['row'=32,'col'=16] {'col'}, dimensions={0}, use_global_device_ids=true | all-gather | bytes 557056 | tf_op jit(solution)/shard_map/all_gather | solution.py:48
  132.0 1.9 while.14
  132.0 0.4 fusion.15
  132.5 0.4 fusion.15
  133.0 0.4 fusion.15
  133.5 0.4 fusion.15
  133.9 1.3 dynamic-slice
  135.9 0.2 dynamic-update-slice
  136.1 35.7 %all-reduce = bf16[512]{0:T(512)(128)(2,1)S(1)} all-reduce(bf16[512]{0:T(512)(128)(2,1)S(1)} %dynamic-update-slice), channel_id=1, replica_groups=mesh['row'=32,'col'=16] {'col'}, use_global_device_ids=true, to_apply=%add | all-reduce | flops 512 | bytes 2048
  171.9 1.1 broadcast_multiply_fusion
  173.0 0.9 copy-done.2
  174.2 0.5 fusion.9
  174.8 1.7 subtract_convert_fusion.1
  176.5 101.8 %reduce-scatter.2.cloned.1.call-done = f32[16,512]{1,0:T(8,128)} async-done(((f32[512,512]{1,0:T(8,128)}), f32[16,512]{1,0:T(8,128)}) %reduce-scatter.2.cloned.1.call-update) | async-done | bytes 32784 | tf_op jit(solution)/shard_map/reduce_scatter | solution.py:70
  278.3 1.4 convert_element_type.45
  (30 shorter events, 1.2 us)
Async XLA Ops:
  7.2 43.8 %copy-start = (bf16[512,512]{1,0:T(8,128)(2,1)S(1)}, bf16[512,512]{1,0:T(8,128)(2,1)}, u32[]{:S(2)}) copy-start(bf16[512,512]{1,0:T(8,128)(2,1)} %param.6) | copy-start | bytes 1572868
  7.2 271.1 %reduce-scatter.2.cloned.1.call-start = ((), (), s32[]{:S(2)}) async-start(), calls=%async_computation.1 | async-start | bytes 1081344 | tf_op jit(solution)/shard_map/reduce_scatter | solution.py:70
  8.5 1.0 copy-start.3
  54.1 0.6 copy-start.4
  133.9 39.1 %copy-start.1 = (bf16[512,512]{1,0:T(8,128)(2,1)}, bf16[512,512]{1,0:T(8,128)(2,1)S(1)}, u32[]{:S(2)}) copy-start(bf16[512,512]{1,0:T(8,128)(2,1)S(1)} %get-tuple-element.195) | copy-start | bytes 1572868
  173.0 0.9 copy-start.2
Sparse Core Ops, SparseCore 0:
  173.1 105.1 reduce-scatter.1
where the time goes:
time: 287 us
  blocking collectives  150 us (52%)
  waiting for transfers between devices  102 us (36%)
  between operations  14.8 us (5%)
  other arithmetic  13.5 us (5%)
  local copies, waits for them, and re-layouts  4.68 us (2%)
    reduce_scatter x1, waiting for transfers between devices, body(): lax.psum_scatter(running * scale_rows[:, None], 'row', scatter_dimension=...  102 us
    pmax x1, blocking collectives, body(): row_peak = lax.pmax(jnp.max(jnp.abs(x_smooth), axis=1), 'row')  47.3 us
    pmax x1, blocking collectives, body(): act_peak, weight_peak = lax.pmax((act_local, weight_local), 'col')  41.3 us
    unnamed x1, blocking collectives  35.7 us
    all_gather x1, blocking collectives, body(): lax.all_gather(local_code, 'col', axis=0, tiled=True)  25.4 us
  transfers between devices with their start and end apart: 1, of which 1 were waited for; matrix products, arithmetic and copies ran while one was open for 1% of the time, Pallas kernels for 0%

commit v1 on v0

--- a/solution.py
+++ b/solution.py
@@ -9,6 +9,11 @@
 EPSILON = 1e-06
 SOFTNESS = 0.9
 TWO_PI = 2.0 * math.pi
+
+
+def all_by_exchange(x, axis, dim):
+    repeated = jnp.stack([x] * lax.axis_size(axis))
+    return jnp.concatenate(lax.all_to_all(repeated, axis, 0, 0), axis=dim)
 
 
 def soften(argument):
@@ -45,7 +50,7 @@
     row_peak = lax.pmax(jnp.max(jnp.abs(x_smooth), axis=1), "row")
     local_code, local_scale = token_encode(x_smooth, row_peak)
     x_code, token_scale = (
-        lax.all_gather(local_code, "col", axis=0, tiled=True),
+        all_by_exchange(local_code, "col", 0),
         lax.all_gather(local_scale, "col", axis=0, tiled=True),
     )
     column_scale = jnp.repeat(query_scale, BLOCK, axis=1)

time: 287 us -> 272 us (0.948)
  blocking collectives: 150 us -> 125 us
  starting transfers between devices: 0.04 us -> 8.05 us
  waiting for transfers between devices: 102 us -> 105 us
    all_gather x1 -> x0, blocking collectives: 25.4 us -> none  [body(): lax.all_gather(local_code, 'col', axis=0, tiled=True)]
    all_to_all x0 -> x1, starting transfers between devices: none -> 8.01 us  [all_by_exchange(): return jnp.concatenate(lax.all_to_all(repeated, axis, 0, 0), axis=dim)]
  transfers between devices with their start and end apart: 1 -> 2, of which waited for: 1 -> 1; matrix products, arithmetic and copies ran while one was open for 1% -> 4% of each run, Pallas kernels for 0% -> 0%
where the time goes in v1:
time: 272 us
  blocking collectives  125 us (46%)
  waiting for transfers between devices  105 us (39%)
  between operations  14.8 us (5%)
  other arithmetic  12.6 us (5%)
  starting transfers between devices  8.05 us (3%)
  local copies, waits for them, and re-layouts  4.72 us (2%)
    reduce_scatter x1, waiting for transfers between devices, body(): lax.psum_scatter(running * scale_rows[:, None], 'row', scatter_dimension=...  105 us
    pmax x1, blocking collectives, body(): row_peak = lax.pmax(jnp.max(jnp.abs(x_smooth), axis=1), 'row')  47.3 us
    pmax x1, blocking collectives, body(): act_peak, weight_peak = lax.pmax((act_local, weight_local), 'col')  41.3 us
    unnamed x1, blocking collectives  36.4 us
    all_to_all x1, starting transfers between devices, all_by_exchange(): return jnp.concatenate(lax.all_to_all(repeated, axis, 0, 0), axis=dim)  8.01 us
    convert_element_type x2, other arithmetic, block_codes(): soften(tile_view / scales[:, None, :, None]).reshape(height, breadth)  5.69 us
  transfers between devices with their start and end apart: 2, of which 1 were waited for; matrix products, arithmetic and copies ran while one was open for 4% of the time, Pallas kernels for 0%

profile of v1, /device:TPU:2, one launch (start us, length us, event | category | flops | bytes accessed | tf_op | source)
XLA Modules:
  0.0 271.8 jit_solution(5406216888413707734)
XLA Ops:
  7.2 1.3 abs_reduce_fusion
  8.6 0.6 copy-done.3
  9.2 41.3 %all-reduce.1 = (f32[512]{0:T(512)S(1)}, f32[512]{0:T(512)S(1)}) all-reduce(f32[512]{0:T(512)S(1)} %maximum_convert_fusion, bf16[512]{0:T(512)(128)(2,1)S(1)} %abs_reduce_fusion.3), channel_id=1, replica_groups=mesh['row'=32,'col'=16] {'col'}, use_global_device_ids=true, to_apply=%region_4.0 | all-reduce | flops 1024 | bytes 7168 | tf_op jit(solution)/shard_map/pmax | solution.py:45
  50.7 47.3 %pmax.23 = f32[32]{0:T(128)S(1)} all-reduce(f32[32]{0:T(128)S(1)} %fusion.6), channel_id=1, replica_groups=mesh['row'=32,'col'=16] {'row'}, use_global_device_ids=true, to_apply=%region_6.0 | all-reduce | flops 32 | bytes 256 | tf_op jit(solution)/shard_map/pmax | solution.py:50
  98.0 0.3 subtract_convert_fusion.2
  98.4 0.8 stack.2
  99.2 8.0 %all-to-all-start = ((bf16[16,32,512]{2,1,0:T(8,128)(2,1)}), bf16[16,32,512]{2,1,0:T(8,128)(2,1)S(1)}, u32[]{:S(2)}, u32[]{:S(2)}) async-start(bf16[16,32,512]{2,1,0:T(8,128)(2,1)} %stack.2), calls=%async_computation | async-start | bytes 1048576 | tf_op jit(solution)/shard_map/all_to_all | solution.py:16
  107.5 1.3 abs.29
  108.8 1.5 reduce_max.65
  110.4 1.3 dynamic-slice
  112.3 0.2 dynamic-update-slice
  112.6 36.4 %all-reduce = bf16[512]{0:T(512)(128)(2,1)S(1)} all-reduce(bf16[512]{0:T(512)(128)(2,1)S(1)} %dynamic-update-slice), channel_id=1, replica_groups=mesh['row'=32,'col'=16] {'col'}, use_global_device_ids=true, to_apply=%add | all-reduce | flops 512 | bytes 2048
  149.2 4.0 %subtract_convert_fusion = bf16[512,512]{1,0:T(8,128)(2,1)S(1)} fusion(f32[64,8,4,128]{3,2,1,0:T(4,128)S(1)} %bitcast.22, bf16[512,512]{1,0:T(8,128)(2,1)S(1)} %copy-done, f32[512]{0:T(512)S(1)} %fusion.7), kind=kLoop, calls=%fused_computation.7 | loop fusion | flops 1835008 | bytes 2099200 | tf_op jit(solution)/shard_map/convert_element_type | solution.py:29
  153.2 1.9 while.14
  153.3 0.4 fusion.15
  153.8 0.4 fusion.15
  154.2 0.4 fusion.15
  154.7 0.4 fusion.15
  155.2 1.2 broadcast_multiply_fusion
  156.3 0.2 abs_reduce_fusion.1
  156.7 0.5 fusion.9
  157.3 1.7 subtract_convert_fusion.1
  158.9 104.6 %reduce-scatter.2.cloned.1.call-done = f32[16,512]{1,0:T(8,128)} async-done(((f32[512,512]{1,0:T(8,128)}), f32[16,512]{1,0:T(8,128)}) %reduce-scatter.2.cloned.1.call-update) | async-done | bytes 32784 | tf_op jit(solution)/shard_map/reduce_scatter | solution.py:75
  263.6 1.4 convert_element_type.45
  (32 shorter events, 1.1 us)
Async XLA Ops:
  7.2 1.3 copy-start.2
  8.4 0.8 copy-start.3
  99.2 8.1 %copy-start = (bf16[512,512]{1,0:T(8,128)(2,1)S(1)}, bf16[512,512]{1,0:T(8,128)(2,1)}, u32[]{:S(2)}) copy-start(bf16[512,512]{1,0:T(8,128)(2,1)} %param.6) | copy-start | bytes 1572868
  99.2 54.0 %all-to-all-start = ((bf16[16,32,512]{2,1,0:T(8,128)(2,1)}), bf16[16,32,512]{2,1,0:T(8,128)(2,1)S(1)}, u32[]{:S(2)}, u32[]{:S(2)}) async-start(bf16[16,32,512]{2,1,0:T(8,128)(2,1)} %stack.2), calls=%async_computation | async-start | bytes 1048576 | tf_op jit(solution)/shard_map/all_to_all | solution.py:16
  107.2 156.3 %reduce-scatter.2.cloned.1.call-start = ((), (), s32[]{:S(2)}) async-start(), calls=%async_computation.2 | async-start | bytes 1081344 | tf_op jit(solution)/shard_map/reduce_scatter | solution.py:75
  110.3 38.7 %copy-start.4 = (f32[4,4]{1,0:T(4,128)}, f32[4,4]{1,0:T(4,128)S(1)}, u32[]{:S(2)}) copy-start(f32[4,4]{1,0:T(4,128)S(1)} %add_multiply_fusion) | copy-start | bytes 196
  155.1 1.2 copy-start.1
Sparse Core Ops, SparseCore 0:
  156.5 107.0 reduce-scatter.1
